TPU v7x, 32 devices: a whole 2x2x4 slice. The times are simulated.
32 devices in a mesh: tm: 8 (over z, core), space: 4 (over y, x).
Axes of the slice: x: 2, y: 2, z: 4, core: 2. Of those that a mesh axis runs over, the one named last changes fastest.
Arguments:
- start_state: float32 [3, 32, 2048], P(None, 'space'), may hold values from -2 to 2
- still_depth: float32 [32, 2048], P('space'), may hold values from 0.25 to 1
- coriolis: float32 [32, 2048], P('space'), may hold values from -0.3 to 0.3
- drag_rate: float32 [32, 2048], P('space'), may hold values from 0.002 to 0.3
Outputs:
- slice_ends: float32 [8, 3, 32, 2048], P('tm', None, 'space')
All inputs are finite; a program needn't handle non-finite values.
Results may differ from a plain program's by a relative error of at most 0.00002.
Values sent between devices are 32-bit elements; how exact they have to be, the bound alone decides.
A program may use at most 64 MiB of HBM per device.

v0:
```python
import jax
import jax.numpy as jnp
from jax import lax
from jax.sharding import PartitionSpec as P

FINE = 4
ITERS = 2


step_len = 1.3


def with_halo(array, sides, width):
    for axis, dim in sides:
        peers, length = (lax.axis_size(axis), array.shape[dim])
        up = [(i, (i + 1) % peers) for i in range(peers)]
        down = [(j, i) for i, j in up]
        last = lax.slice_in_dim(array, length - width, length, axis=dim)
        initial = lax.slice_in_dim(array, 0, width, axis=dim)
        before = lax.ppermute(last, axis, up)
        after = lax.ppermute(initial, axis, down)
        array = jnp.concatenate([before, array, after], axis=dim)
    return array


def carried_in(part, axis, combine, identity):
    place = lax.axis_index(axis)
    gathered = jax.tree.map(lambda a: lax.all_gather(a, axis), part)
    state = jax.tree.map(lambda a, e: jnp.zeros_like(a) + jnp.asarray(e, a.dtype), part, identity)

    def one(lap, state):
        return combine(
            state, jax.tree.map(lambda a: lax.dynamic_index_in_dim(a, lap, 0, False), gathered)
        )

    return lax.fori_loop(0, place, one, state)


def coarse_power(steps_done, decay_total, turn_angle):
    damping = jnp.exp(-steps_done * decay_total)
    return (damping * jnp.cos(steps_done * turn_angle), -damping * jnp.sin(steps_done * turn_angle))


def rotate(fields, part_re, part_im):
    height = fields[..., 0, :, :]
    along_x = fields[..., 1, :, :]
    along_y = fields[..., 2, :, :]
    turned_x = part_re * along_x - part_im * along_y
    turned_y = part_im * along_x + part_re * along_y
    return jnp.stack([height, turned_x, turned_y], axis=-3)


def step_margins(fields, still_depth, cosine, sine_step, damping):
    height = fields[0]
    along_x = fields[1]
    along_y = fields[2]
    flux_x = still_depth * along_x
    flux_y = still_depth * along_y
    padded = with_halo(flux_x, (("space", 0),), 1)
    divergence = (padded[2:] - padded[:-2]) * 0.5 + (
        jnp.roll(flux_y, -1, 1) - jnp.roll(flux_y, 1, 1)
    ) * 0.5
    height_new = height - step_len * divergence
    height_pad = with_halo(height_new, (("space", 0),), 1)
    slope_x = (height_pad[2:] - height_pad[:-2]) * 0.5
    slope_y = (jnp.roll(height_new, -1, 1) - jnp.roll(height_new, 1, 1)) * 0.5
    new_x = damping * (cosine * along_x + sine_step * along_y) - step_len * slope_x
    new_y = damping * (cosine * along_y - sine_step * along_x) - step_len * slope_y
    return jnp.stack([height_new, new_x, new_y])


def on_device(start_state, still_depth, coriolis, drag_rate):
    turn_angle = FINE * step_len * coriolis
    decay_total = FINE * drag_rate
    cosine = jnp.cos(step_len * coriolis)
    sine_step = jnp.sin(step_len * coriolis)
    damping = jnp.exp(-drag_rate)
    slice_index = lax.axis_index("tm").astype(jnp.float32)
    power_re, power_im = coarse_power(slice_index, decay_total, turn_angle)
    fields = rotate(start_state, power_re, power_im)
    coarse_re, coarse_im = coarse_power(1.0, decay_total, turn_angle)

    def combine_maps(first_map, second_map):
        re_one, im_one, bh_one, bx_one, by_one = first_map
        re_two, im_two, bh_two, bx_two, by_two = second_map
        return (
            re_two * re_one - im_two * im_one,
            re_two * im_one + im_two * re_one,
            bh_one + bh_two,
            re_two * bx_one - im_two * by_one + bx_two,
            im_two * bx_one + re_two * by_one + by_two,
        )

    zeros_cell = jnp.zeros_like(still_depth)
    slice_ends = fields
    for repeat in range(ITERS):
        fine_end = fields
        for inner in range(FINE):
            fine_end = step_margins(fine_end, still_depth, cosine, sine_step, damping)
        jump_terms = fine_end - rotate(fields, coarse_re, coarse_im)
        elements = (coarse_re, coarse_im, jump_terms[0], jump_terms[1], jump_terms[2])
        identity_map = (jnp.ones_like(still_depth), zeros_cell, zeros_cell, zeros_cell, zeros_cell)
        prefix_re, prefix_im, shift_h, shift_x, shift_y = carried_in(
            elements, "tm", combine_maps, identity_map
        )
        updated_h = start_state[0] + shift_h
        updated_x = prefix_re * start_state[1] - prefix_im * start_state[2] + shift_x
        updated_y = prefix_im * start_state[1] + prefix_re * start_state[2] + shift_y
        fields = jnp.stack([updated_h, updated_x, updated_y])
        slice_ends = rotate(fields, coarse_re, coarse_im) + jump_terms
    return slice_ends[None]


def solution(mesh):
    placed = (P(None, "space", None), P("space", None), P("space", None), P("space", None))
    return jax.shard_map(
        on_device,
        mesh=mesh,
        in_specs=placed,
        out_specs=P("tm", None, "space", None),
        check_vma=False,
    )
```

profile of v0, /device:TPU:25, one launch (start us, length us, event | category | flops | bytes accessed | tf_op | source)
XLA Modules:
  0.0 216.3 jit_solution(16390283981923862269)
XLA Ops:
  0.0 1.5 subtract_bitcast_fusion.1
  1.5 2.2 %collective-permute-start = (f32[1,2048]{1,0:T(1,128)S(1)}, f32[1,2048]{1,0:T(1,128)S(1)}, u32[]{:S(2)}, u32[]{:S(2)}) collective-permute-start(f32[1,2048]{1,0:T(1,128)S(1)} %get-tuple-element.360), channel_id=1, source_target_pairs={{1,0},{2,1},{3,2},{0,3},{5,4},{6,5},{7,6},{4,7},{9,8},{10,9},{11,1... | collective-permute-start | bytes 24584 | tf_op jit(solution)/shard_map/ppermute | solution.py:21
  3.8 15.7 %all-gather.1 = f32[64,2048]{1,0:T(8,128)S(1)} all-gather(f32[8,2048]{1,0:T(8,128)S(1)} %get-tuple-element.214), channel_id=3, replica_groups=mesh['tm'=8,'space'=4] {'tm'}, dimensions={0}, use_global_device_ids=true | all-gather | bytes 589824 | tf_op jit(solution)/shard_map/all_gather | solution.py:28
  19.5 15.2 %all-gather = f32[64,2048]{1,0:T(8,128)S(1)} all-gather(f32[8,2048]{1,0:T(8,128)S(1)} %get-tuple-element.215), channel_id=2, replica_groups=mesh['tm'=8,'space'=4] {'tm'}, dimensions={0}, use_global_device_ids=true | all-gather | bytes 589824 | tf_op jit(solution)/shard_map/all_gather | solution.py:28
  35.0 2.6 %collective-permute-start.2 = (f32[1,2048]{1,0:T(1,128)S(1)}, f32[1,2048]{1,0:T(1,128)S(1)}, u32[]{:S(2)}, u32[]{:S(2)}) collective-permute-start(f32[1,2048]{1,0:T(1,128)S(1)} %get-tuple-element.352), channel_id=1, source_target_pairs={{1,0},{2,1},{3,2},{0,3},{5,4},{6,5},{7,6},{4,7},{9,8},{10,9},{11,1... | collective-permute-start | bytes 24584 | tf_op jit(solution)/shard_map/ppermute | solution.py:21
  38.4 2.6 %collective-permute-done.3 = f32[1,2048]{1,0:T(1,128)S(1)} collective-permute-done((f32[1,2048]{1,0:T(1,128)S(1)}, f32[1,2048]{1,0:T(1,128)S(1)}, u32[]{:S(2)}, u32[]{:S(2)}) %collective-permute-start.3) | collective-permute-done | bytes 8224 | tf_op jit(solution)/shard_map/ppermute | solution.py:20
  41.5 1.5 collective-permute-start.5
  47.6 1.3 collective-permute-done.7
  51.9 1.3 collective-permute-done.9
  53.5 1.4 collective-permute-start.10
  56.0 2.3 %collective-permute-done.11 = f32[1,2048]{1,0:T(1,128)S(1)} collective-permute-done((f32[1,2048]{1,0:T(1,128)S(1)}, f32[1,2048]{1,0:T(1,128)S(1)}, u32[]{:S(2)}, u32[]{:S(2)}) %collective-permute-start.11) | collective-permute-done | bytes 8224 | tf_op jit(solution)/shard_map/ppermute | solution.py:20
  58.8 1.4 collective-permute-start.13
  62.5 1.3 collective-permute-start.15
  66.8 25.0 %all_gather.40 = f32[8,8,2048]{2,1,0:T(8,128)S(1)} all-gather(f32[1,8,2048]{2,1,0:T(8,128)S(1)} %get-tuple-element.257), channel_id=1, replica_groups=mesh['tm'=8,'space'=4] {'tm'}, dimensions={0}, use_global_device_ids=true | all-gather | bytes 589824 | tf_op jit(solution)/shard_map/all_gather | solution.py:28
  91.8 15.1 %all_gather.39 = f32[8,8,2048]{2,1,0:T(8,128)S(1)} all-gather(f32[1,8,2048]{2,1,0:T(8,128)S(1)} %get-tuple-element.258), channel_id=1, replica_groups=mesh['tm'=8,'space'=4] {'tm'}, dimensions={0}, use_global_device_ids=true | all-gather | bytes 589824 | tf_op jit(solution)/shard_map/all_gather | solution.py:28
  106.9 15.1 %all_gather.38 = f32[8,8,2048]{2,1,0:T(8,128)S(1)} all-gather(f32[1,8,2048]{2,1,0:T(8,128)S(1)} %get-tuple-element.259), channel_id=1, replica_groups=mesh['tm'=8,'space'=4] {'tm'}, dimensions={0}, use_global_device_ids=true | all-gather | bytes 589824 | tf_op jit(solution)/shard_map/all_gather | solution.py:28
  123.1 1.5 collective-permute-start.17
  127.4 1.4 collective-permute-start.18
  129.9 2.3 %collective-permute-done.19 = f32[1,2048]{1,0:T(1,128)S(1)} collective-permute-done((f32[1,2048]{1,0:T(1,128)S(1)}, f32[1,2048]{1,0:T(1,128)S(1)}, u32[]{:S(2)}, u32[]{:S(2)}) %collective-permute-start.19) | collective-permute-done | bytes 8224 | tf_op jit(solution)/shard_map/ppermute | solution.py:20
  132.6 1.4 collective-permute-start.21
  137.8 1.1 collective-permute-done.22
  138.8 1.4 collective-permute-done.23
  140.9 1.2 collective-permute-start.25
  143.2 1.1 collective-permute-done.25
  144.6 1.2 collective-permute-start.26
  147.1 2.0 collective-permute-done.27
  149.9 1.1 collective-permute-start.29
  152.1 1.2 collective-permute-done.29
  156.0 1.5 collective-permute-done.31
  157.9 25.9 %all_gather.43 = f32[8,8,2048]{2,1,0:T(8,128)S(1)} all-gather(f32[1,8,2048]{2,1,0:T(8,128)S(1)} %get-tuple-element.254), channel_id=1, replica_groups=mesh['tm'=8,'space'=4] {'tm'}, dimensions={0}, use_global_device_ids=true | all-gather | bytes 589824 | tf_op jit(solution)/shard_map/all_gather | solution.py:28
  183.8 15.1 %all_gather.42 = f32[8,8,2048]{2,1,0:T(8,128)S(1)} all-gather(f32[1,8,2048]{2,1,0:T(8,128)S(1)} %get-tuple-element.255), channel_id=1, replica_groups=mesh['tm'=8,'space'=4] {'tm'}, dimensions={0}, use_global_device_ids=true | all-gather | bytes 589824 | tf_op jit(solution)/shard_map/all_gather | solution.py:28
  198.9 15.1 %all_gather.41 = f32[8,8,2048]{2,1,0:T(8,128)S(1)} all-gather(f32[1,8,2048]{2,1,0:T(8,128)S(1)} %get-tuple-element.256), channel_id=1, replica_groups=mesh['tm'=8,'space'=4] {'tm'}, dimensions={0}, use_global_device_ids=true | all-gather | bytes 589824 | tf_op jit(solution)/shard_map/all_gather | solution.py:28
  (161 shorter events, 37.0 us)
Async XLA Ops:
  1.5 33.3 %collective-permute-start = (f32[1,2048]{1,0:T(1,128)S(1)}, f32[1,2048]{1,0:T(1,128)S(1)}, u32[]{:S(2)}, u32[]{:S(2)}) collective-permute-start(f32[1,2048]{1,0:T(1,128)S(1)} %get-tuple-element.360), channel_id=1, source_target_pairs={{1,0},{2,1},{3,2},{0,3},{5,4},{6,5},{7,6},{4,7},{9,8},{10,9},{11,1... | collective-permute-start | bytes 24584 | tf_op jit(solution)/shard_map/ppermute | solution.py:21
  3.8 31.1 %collective-permute-start.1 = (f32[1,2048]{1,0:T(1,128)S(1)}, f32[1,2048]{1,0:T(1,128)S(1)}, u32[]{:S(2)}, u32[]{:S(2)}) collective-permute-start(f32[1,2048]{1,0:T(1,128)S(1)} %get-tuple-element.361), channel_id=1, source_target_pairs={{0,1},{1,2},{2,3},{3,0},{4,5},{5,6},{6,7},{7,4},{8,9},{9,10},{10,1... | collective-permute-start | bytes 24584 | tf_op jit(solution)/shard_map/ppermute | solution.py:20
  35.0 3.4 %collective-permute-start.2 = (f32[1,2048]{1,0:T(1,128)S(1)}, f32[1,2048]{1,0:T(1,128)S(1)}, u32[]{:S(2)}, u32[]{:S(2)}) collective-permute-start(f32[1,2048]{1,0:T(1,128)S(1)} %get-tuple-element.352), channel_id=1, source_target_pairs={{1,0},{2,1},{3,2},{0,3},{5,4},{6,5},{7,6},{4,7},{9,8},{10,9},{11,1... | collective-permute-start | bytes 24584 | tf_op jit(solution)/shard_map/ppermute | solution.py:21
  37.6 3.4 %collective-permute-start.3 = (f32[1,2048]{1,0:T(1,128)S(1)}, f32[1,2048]{1,0:T(1,128)S(1)}, u32[]{:S(2)}, u32[]{:S(2)}) collective-permute-start(f32[1,2048]{1,0:T(1,128)S(1)} %get-tuple-element.353), channel_id=1, source_target_pairs={{0,1},{1,2},{2,3},{3,0},{4,5},{5,6},{6,7},{7,4},{8,9},{9,10},{10,1... | collective-permute-start | bytes 24584 | tf_op jit(solution)/shard_map/ppermute | solution.py:20
  41.4 2.6 %collective-permute-start.4 = (f32[1,2048]{1,0:T(1,128)S(1)}, f32[1,2048]{1,0:T(1,128)S(1)}, u32[]{:S(2)}, u32[]{:S(2)}) collective-permute-start(f32[1,2048]{1,0:T(1,128)S(1)} %get-tuple-element.350), channel_id=1, source_target_pairs={{1,0},{2,1},{3,2},{0,3},{5,4},{6,5},{7,6},{4,7},{9,8},{10,9},{11,1... | collective-permute-start | bytes 24584 | tf_op jit(solution)/shard_map/ppermute | solution.py:21
  41.5 3.5 %collective-permute-start.5 = (f32[1,2048]{1,0:T(1,128)S(1)}, f32[1,2048]{1,0:T(1,128)S(1)}, u32[]{:S(2)}, u32[]{:S(2)}) collective-permute-start(f32[1,2048]{1,0:T(1,128)S(1)} %get-tuple-element.351), channel_id=1, source_target_pairs={{0,1},{1,2},{2,3},{3,0},{4,5},{5,6},{6,7},{7,4},{8,9},{9,10},{10,1... | collective-permute-start | bytes 24584 | tf_op jit(solution)/shard_map/ppermute | solution.py:20
  45.1 2.5 %collective-permute-start.6 = (f32[1,2048]{1,0:T(1,128)S(1)}, f32[1,2048]{1,0:T(1,128)S(1)}, u32[]{:S(2)}, u32[]{:S(2)}) collective-permute-start(f32[1,2048]{1,0:T(1,128)S(1)} %get-tuple-element.340), channel_id=1, source_target_pairs={{1,0},{2,1},{3,2},{0,3},{5,4},{6,5},{7,6},{4,7},{9,8},{10,9},{11,1... | collective-permute-start | bytes 24584 | tf_op jit(solution)/shard_map/ppermute | solution.py:21
  45.6 3.4 %collective-permute-start.7 = (f32[1,2048]{1,0:T(1,128)S(1)}, f32[1,2048]{1,0:T(1,128)S(1)}, u32[]{:S(2)}, u32[]{:S(2)}) collective-permute-start(f32[1,2048]{1,0:T(1,128)S(1)} %get-tuple-element.341), channel_id=1, source_target_pairs={{0,1},{1,2},{2,3},{3,0},{4,5},{5,6},{6,7},{7,4},{8,9},{9,10},{10,1... | collective-permute-start | bytes 24584 | tf_op jit(solution)/shard_map/ppermute | solution.py:20
  49.3 2.6 %collective-permute-start.8 = (f32[1,2048]{1,0:T(1,128)S(1)}, f32[1,2048]{1,0:T(1,128)S(1)}, u32[]{:S(2)}, u32[]{:S(2)}) collective-permute-start(f32[1,2048]{1,0:T(1,128)S(1)} %get-tuple-element.338), channel_id=1, source_target_pairs={{1,0},{2,1},{3,2},{0,3},{5,4},{6,5},{7,6},{4,7},{9,8},{10,9},{11,1... | collective-permute-start | bytes 24584 | tf_op jit(solution)/shard_map/ppermute | solution.py:21
  49.8 3.4 %collective-permute-start.9 = (f32[1,2048]{1,0:T(1,128)S(1)}, f32[1,2048]{1,0:T(1,128)S(1)}, u32[]{:S(2)}, u32[]{:S(2)}) collective-permute-start(f32[1,2048]{1,0:T(1,128)S(1)} %get-tuple-element.339), channel_id=1, source_target_pairs={{0,1},{1,2},{2,3},{3,0},{4,5},{5,6},{6,7},{7,4},{8,9},{9,10},{10,1... | collective-permute-start | bytes 24584 | tf_op jit(solution)/shard_map/ppermute | solution.py:20
  53.5 2.5 %collective-permute-start.10 = (f32[1,2048]{1,0:T(1,128)S(1)}, f32[1,2048]{1,0:T(1,128)S(1)}, u32[]{:S(2)}, u32[]{:S(2)}) collective-permute-start(f32[1,2048]{1,0:T(1,128)S(1)} %get-tuple-element.328), channel_id=1, source_target_pairs={{1,0},{2,1},{3,2},{0,3},{5,4},{6,5},{7,6},{4,7},{9,8},{10,9},{11,1... | collective-permute-start | bytes 24584 | tf_op jit(solution)/shard_map/ppermute | solution.py:21
  54.9 3.4 %collective-permute-start.11 = (f32[1,2048]{1,0:T(1,128)S(1)}, f32[1,2048]{1,0:T(1,128)S(1)}, u32[]{:S(2)}, u32[]{:S(2)}) collective-permute-start(f32[1,2048]{1,0:T(1,128)S(1)} %get-tuple-element.329), channel_id=1, source_target_pairs={{0,1},{1,2},{2,3},{3,0},{4,5},{5,6},{6,7},{7,4},{8,9},{9,10},{10,1... | collective-permute-start | bytes 24584 | tf_op jit(solution)/shard_map/ppermute | solution.py:20
  58.6 2.6 %collective-permute-start.12 = (f32[1,2048]{1,0:T(1,128)S(1)}, f32[1,2048]{1,0:T(1,128)S(1)}, u32[]{:S(2)}, u32[]{:S(2)}) collective-permute-start(f32[1,2048]{1,0:T(1,128)S(1)} %get-tuple-element.326), channel_id=1, source_target_pairs={{1,0},{2,1},{3,2},{0,3},{5,4},{6,5},{7,6},{4,7},{9,8},{10,9},{11,1... | collective-permute-start | bytes 24584 | tf_op jit(solution)/shard_map/ppermute | solution.py:21
  58.8 3.4 %collective-permute-start.13 = (f32[1,2048]{1,0:T(1,128)S(1)}, f32[1,2048]{1,0:T(1,128)S(1)}, u32[]{:S(2)}, u32[]{:S(2)}) collective-permute-start(f32[1,2048]{1,0:T(1,128)S(1)} %get-tuple-element.327), channel_id=1, source_target_pairs={{0,1},{1,2},{2,3},{3,0},{4,5},{5,6},{6,7},{7,4},{8,9},{9,10},{10,1... | collective-permute-start | bytes 24584 | tf_op jit(solution)/shard_map/ppermute | solution.py:20
  62.4 2.5 %collective-permute-start.14 = (f32[1,2048]{1,0:T(1,128)S(1)}, f32[1,2048]{1,0:T(1,128)S(1)}, u32[]{:S(2)}, u32[]{:S(2)}) collective-permute-start(f32[1,2048]{1,0:T(1,128)S(1)} %get-tuple-element.312), channel_id=1, source_target_pairs={{1,0},{2,1},{3,2},{0,3},{5,4},{6,5},{7,6},{4,7},{9,8},{10,9},{11,1... | collective-permute-start | bytes 24584 | tf_op jit(solution)/shard_map/ppermute | solution.py:21
  62.5 3.4 %collective-permute-start.15 = (f32[1,2048]{1,0:T(1,128)S(1)}, f32[1,2048]{1,0:T(1,128)S(1)}, u32[]{:S(2)}, u32[]{:S(2)}) collective-permute-start(f32[1,2048]{1,0:T(1,128)S(1)} %get-tuple-element.313), channel_id=1, source_target_pairs={{0,1},{1,2},{2,3},{3,0},{4,5},{5,6},{6,7},{7,4},{8,9},{9,10},{10,1... | collective-permute-start | bytes 24584 | tf_op jit(solution)/shard_map/ppermute | solution.py:20
  123.0 2.6 %collective-permute-start.16 = (f32[1,2048]{1,0:T(1,128)S(1)}, f32[1,2048]{1,0:T(1,128)S(1)}, u32[]{:S(2)}, u32[]{:S(2)}) collective-permute-start(f32[1,2048]{1,0:T(1,128)S(1)} %get-tuple-element.310), channel_id=1, source_target_pairs={{1,0},{2,1},{3,2},{0,3},{5,4},{6,5},{7,6},{4,7},{9,8},{10,9},{11,1... | collective-permute-start | bytes 24584 | tf_op jit(solution)/shard_map/ppermute | solution.py:21
  123.1 3.5 %collective-permute-start.17 = (f32[1,2048]{1,0:T(1,128)S(1)}, f32[1,2048]{1,0:T(1,128)S(1)}, u32[]{:S(2)}, u32[]{:S(2)}) collective-permute-start(f32[1,2048]{1,0:T(1,128)S(1)} %get-tuple-element.311), channel_id=1, source_target_pairs={{0,1},{1,2},{2,3},{3,0},{4,5},{5,6},{6,7},{7,4},{8,9},{9,10},{10,1... | collective-permute-start | bytes 24584 | tf_op jit(solution)/shard_map/ppermute | solution.py:20
  127.4 2.5 %collective-permute-start.18 = (f32[1,2048]{1,0:T(1,128)S(1)}, f32[1,2048]{1,0:T(1,128)S(1)}, u32[]{:S(2)}, u32[]{:S(2)}) collective-permute-start(f32[1,2048]{1,0:T(1,128)S(1)} %get-tuple-element.302), channel_id=1, source_target_pairs={{1,0},{2,1},{3,2},{0,3},{5,4},{6,5},{7,6},{4,7},{9,8},{10,9},{11,1... | collective-permute-start | bytes 24584 | tf_op jit(solution)/shard_map/ppermute | solution.py:21
  128.8 3.4 %collective-permute-start.19 = (f32[1,2048]{1,0:T(1,128)S(1)}, f32[1,2048]{1,0:T(1,128)S(1)}, u32[]{:S(2)}, u32[]{:S(2)}) collective-permute-start(f32[1,2048]{1,0:T(1,128)S(1)} %get-tuple-element.303), channel_id=1, source_target_pairs={{0,1},{1,2},{2,3},{3,0},{4,5},{5,6},{6,7},{7,4},{8,9},{9,10},{10,1... | collective-permute-start | bytes 24584 | tf_op jit(solution)/shard_map/ppermute | solution.py:20
  132.5 2.6 %collective-permute-start.20 = (f32[1,2048]{1,0:T(1,128)S(1)}, f32[1,2048]{1,0:T(1,128)S(1)}, u32[]{:S(2)}, u32[]{:S(2)}) collective-permute-start(f32[1,2048]{1,0:T(1,128)S(1)} %get-tuple-element.300), channel_id=1, source_target_pairs={{1,0},{2,1},{3,2},{0,3},{5,4},{6,5},{7,6},{4,7},{9,8},{10,9},{11,1... | collective-permute-start | bytes 24584 | tf_op jit(solution)/shard_map/ppermute | solution.py:21
  132.6 3.4 %collective-permute-start.21 = (f32[1,2048]{1,0:T(1,128)S(1)}, f32[1,2048]{1,0:T(1,128)S(1)}, u32[]{:S(2)}, u32[]{:S(2)}) collective-permute-start(f32[1,2048]{1,0:T(1,128)S(1)} %get-tuple-element.301), channel_id=1, source_target_pairs={{0,1},{1,2},{2,3},{3,0},{4,5},{5,6},{6,7},{7,4},{8,9},{9,10},{10,1... | collective-permute-start | bytes 24584 | tf_op jit(solution)/shard_map/ppermute | solution.py:20
  136.2 2.6 %collective-permute-start.22 = (f32[1,2048]{1,0:T(1,128)S(1)}, f32[1,2048]{1,0:T(1,128)S(1)}, u32[]{:S(2)}, u32[]{:S(2)}) collective-permute-start(f32[1,2048]{1,0:T(1,128)S(1)} %get-tuple-element.290), channel_id=1, source_target_pairs={{1,0},{2,1},{3,2},{0,3},{5,4},{6,5},{7,6},{4,7},{9,8},{10,9},{11,1... | collective-permute-start | bytes 24584 | tf_op jit(solution)/shard_map/ppermute | solution.py:21
  136.9 3.4 %collective-permute-start.23 = (f32[1,2048]{1,0:T(1,128)S(1)}, f32[1,2048]{1,0:T(1,128)S(1)}, u32[]{:S(2)}, u32[]{:S(2)}) collective-permute-start(f32[1,2048]{1,0:T(1,128)S(1)} %get-tuple-element.291), channel_id=1, source_target_pairs={{0,1},{1,2},{2,3},{3,0},{4,5},{5,6},{6,7},{7,4},{8,9},{9,10},{10,1... | collective-permute-start | bytes 24584 | tf_op jit(solution)/shard_map/ppermute | solution.py:20
  140.6 2.6 %collective-permute-start.24 = (f32[1,2048]{1,0:T(1,128)S(1)}, f32[1,2048]{1,0:T(1,128)S(1)}, u32[]{:S(2)}, u32[]{:S(2)}) collective-permute-start(f32[1,2048]{1,0:T(1,128)S(1)} %get-tuple-element.288), channel_id=1, source_target_pairs={{1,0},{2,1},{3,2},{0,3},{5,4},{6,5},{7,6},{4,7},{9,8},{10,9},{11,1... | collective-permute-start | bytes 24584 | tf_op jit(solution)/shard_map/ppermute | solution.py:21
  140.9 3.4 %collective-permute-start.25 = (f32[1,2048]{1,0:T(1,128)S(1)}, f32[1,2048]{1,0:T(1,128)S(1)}, u32[]{:S(2)}, u32[]{:S(2)}) collective-permute-start(f32[1,2048]{1,0:T(1,128)S(1)} %get-tuple-element.289), channel_id=1, source_target_pairs={{0,1},{1,2},{2,3},{3,0},{4,5},{5,6},{6,7},{7,4},{8,9},{9,10},{10,1... | collective-permute-start | bytes 24584 | tf_op jit(solution)/shard_map/ppermute | solution.py:20
  144.6 2.5 %collective-permute-start.26 = (f32[1,2048]{1,0:T(1,128)S(1)}, f32[1,2048]{1,0:T(1,128)S(1)}, u32[]{:S(2)}, u32[]{:S(2)}) collective-permute-start(f32[1,2048]{1,0:T(1,128)S(1)} %get-tuple-element.278), channel_id=1, source_target_pairs={{1,0},{2,1},{3,2},{0,3},{5,4},{6,5},{7,6},{4,7},{9,8},{10,9},{11,1... | collective-permute-start | bytes 24584 | tf_op jit(solution)/shard_map/ppermute | solution.py:21
  145.7 3.4 %collective-permute-start.27 = (f32[1,2048]{1,0:T(1,128)S(1)}, f32[1,2048]{1,0:T(1,128)S(1)}, u32[]{:S(2)}, u32[]{:S(2)}) collective-permute-start(f32[1,2048]{1,0:T(1,128)S(1)} %get-tuple-element.279), channel_id=1, source_target_pairs={{0,1},{1,2},{2,3},{3,0},{4,5},{5,6},{6,7},{7,4},{8,9},{9,10},{10,1... | collective-permute-start | bytes 24584 | tf_op jit(solution)/shard_map/ppermute | solution.py:20
  149.5 2.6 %collective-permute-start.28 = (f32[1,2048]{1,0:T(1,128)S(1)}, f32[1,2048]{1,0:T(1,128)S(1)}, u32[]{:S(2)}, u32[]{:S(2)}) collective-permute-start(f32[1,2048]{1,0:T(1,128)S(1)} %get-tuple-element.276), channel_id=1, source_target_pairs={{1,0},{2,1},{3,2},{0,3},{5,4},{6,5},{7,6},{4,7},{9,8},{10,9},{11,1... | collective-permute-start | bytes 24584 | tf_op jit(solution)/shard_map/ppermute | solution.py:21
  149.9 3.4 %collective-permute-start.29 = (f32[1,2048]{1,0:T(1,128)S(1)}, f32[1,2048]{1,0:T(1,128)S(1)}, u32[]{:S(2)}, u32[]{:S(2)}) collective-permute-start(f32[1,2048]{1,0:T(1,128)S(1)} %get-tuple-element.277), channel_id=1, source_target_pairs={{0,1},{1,2},{2,3},{3,0},{4,5},{5,6},{6,7},{7,4},{8,9},{9,10},{10,1... | collective-permute-start | bytes 24584 | tf_op jit(solution)/shard_map/ppermute | solution.py:20
  153.5 2.5 %collective-permute-start.30 = (f32[1,2048]{1,0:T(1,128)S(1)}, f32[1,2048]{1,0:T(1,128)S(1)}, u32[]{:S(2)}, u32[]{:S(2)}) collective-permute-start(f32[1,2048]{1,0:T(1,128)S(1)} %get-tuple-element.262), channel_id=1, source_target_pairs={{1,0},{2,1},{3,2},{0,3},{5,4},{6,5},{7,6},{4,7},{9,8},{10,9},{11,1... | collective-permute-start | bytes 24584 | tf_op jit(solution)/shard_map/ppermute | solution.py:21
  154.1 3.4 %collective-permute-start.31 = (f32[1,2048]{1,0:T(1,128)S(1)}, f32[1,2048]{1,0:T(1,128)S(1)}, u32[]{:S(2)}, u32[]{:S(2)}) collective-permute-start(f32[1,2048]{1,0:T(1,128)S(1)} %get-tuple-element.263), channel_id=1, source_target_pairs={{0,1},{1,2},{2,3},{3,0},{4,5},{5,6},{6,7},{7,4},{8,9},{9,10},{10,1... | collective-permute-start | bytes 24584 | tf_op jit(solution)/shard_map/ppermute | solution.py:20
  (9 other events, 57.8 us)
where the time goes:
time: 217 us; the launch traced here: 216 us
  blocking collectives  142 us (65%)
  waiting for transfers between devices  35.4 us (16%)
  starting transfers between devices  25.9 us (12%)
  other arithmetic  7.95 us (4%)
  local copies, waits for them, and re-layouts  4.33 us (2%)
    all_gather x8, blocking collectives, carried_in(): gathered = jax.tree.map(lambda a: lax.all_gather(a, axis), part)  142 us
    ppermute x16, waiting for transfers between devices, with_halo(): before = lax.ppermute(last, axis, up)  22.2 us
    ppermute x16, starting transfers between devices, with_halo(): before = lax.ppermute(last, axis, up)  13.6 us
    ppermute x16, waiting for transfers between devices, with_halo(): after = lax.ppermute(initial, axis, down)  13.2 us
    ppermute x16, starting transfers between devices, with_halo(): after = lax.ppermute(initial, axis, down)  12.3 us
  transfers between devices with their start and end apart: 32, of which 30 were waited for; matrix products, arithmetic and copies ran while one was open for 1% of the time, Pallas kernels for 0%

commit v1 on v0

v1 whole, which is shorter than its diff:
```python
import functools

import jax
import jax.numpy as jnp
from jax import lax
from jax.experimental import pallas as pl
from jax.experimental.pallas import tpu as pltpu
from jax.sharding import PartitionSpec as P

FINE = 4
ITERS = 2

step_len = 1.3
half_step = 0.5 * step_len

LANES = 128
SUBLANES = 8
MESH = pl.DeviceIdType.MESH


def members_of(tm, space, columns):
    best = 1
    for count in range(1, tm + 1):
        if tm % count == 0 and columns % (space * count * LANES) == 0:
            best = count
    return best


def kernel(
    sizes, start_ref, depth_ref, coriolis_ref, drag_ref, out_ref,
    state_in, depth_in, coriolis_in, drag_in, stage, recv, coefs, ahead, current, ends, outgoing,
    load_sem, in_send, in_recv, out_send, out_recv,
):
    tm_size, space, members, strip, columns = sizes
    width = columns // (space * members)
    tiles = width // LANES
    lanes = width + LANES
    rows = space * strip
    groups_of_rows = rows // SUBLANES
    peers = space * members
    fields = 6

    time = lax.axis_index("tm")
    place = lax.axis_index("space")
    group = lax.div(time, members)
    member = lax.rem(time, members)
    block = member * space + place

    loads = [
        pltpu.make_async_copy(src, dst, load_sem.at[i])
        for i, (src, dst) in enumerate(
            ((start_ref, state_in), (depth_ref, depth_in), (coriolis_ref, coriolis_in), (drag_ref, drag_in))
        )
    ]
    for load in loads:
        load.start()

    barrier = pltpu.get_barrier_semaphore()
    for away in range(1, peers):
        peer = lax.rem(block + away, peers)
        pl.semaphore_signal(
            barrier, inc=1,
            device_id=(group * members + lax.div(peer, space), lax.rem(peer, space)),
            device_id_type=MESH,
        )
    for load in loads:
        load.wait()

    lane = lax.broadcasted_iota(jnp.int32, (strip, LANES), 1)
    spread = LANES // 4
    for k in range(space):
        base = (member * space + k) * width
        offsets = [base + t * LANES for t in range(tiles)]
        before = lax.rem(base + columns - LANES, columns)
        after = lax.rem(base + width, columns)

        def tile(ref, index, offset):
            window = pl.ds(pl.multiple_of(offset, LANES), LANES)
            return ref[:, window] if index is None else ref[index, :, window]

        def pieces(ref, index=None):
            halo = jnp.where(lane < LANES // 2, tile(ref, index, after), tile(ref, index, before))
            return [tile(ref, index, offset) for offset in offsets] + [halo]

        height, along_x, along_y = [pieces(state_in, f) for f in range(3)]
        height = [half_step * a for a in height]
        depth = [(half_step * half_step) * a for a in pieces(depth_in)]
        angle = [step_len * a for a in pieces(coriolis_in)]
        damping = [jnp.exp(-a) for a in pieces(drag_in)]
        cosine = [d * jnp.cos(a) for d, a in zip(damping, angle)]
        sine = [d * jnp.sin(a) for d, a in zip(damping, angle)]
        everything = (height, along_x, along_y, depth, cosine, sine)
        for f, parts in enumerate(everything):
            for t in range(tiles):
                stage[k, f * tiles + t] = parts[t]
        for first in range(0, fields, 4):
            packed = everything[first][-1]
            for f in range(first + 1, min(first + 4, fields)):
                moved = pltpu.roll(everything[f][-1], spread * (f - first), 1)
                low = spread * (f - first) - spread // 2
                packed = jnp.where((lane >= low) & (lane < low + spread), moved, packed)
            stage[k, fields * tiles + first // 4] = packed

    recv[:, pl.ds(pl.multiple_of(place * strip, strip), strip), :] = stage[place]

    pl.semaphore_wait(barrier, peers - 1)

    def strip_copy(target, source):
        return pltpu.make_async_remote_copy(
            src_ref=stage.at[target],
            dst_ref=recv.at[:, pl.ds(pl.multiple_of(source * strip, strip), strip), :],
            send_sem=in_send.at[target],
            recv_sem=in_recv.at[source],
            device_id=(time, target),
            device_id_type=MESH,
        )

    others = [lax.rem(place + away, space) for away in range(1, space)]
    for k in others:
        strip_copy(k, place).start()
    for k in others:
        strip_copy(k, k).wait_recv()

    def slab(tile_index, j):
        return recv[tile_index, pl.ds(j, SUBLANES, stride=groups_of_rows), :]

    for j in range(groups_of_rows):
        whole = []
        for f in range(fields):
            parts = [slab(f * tiles + t, j) for t in range(tiles)]
            halo = slab(fields * tiles + f // 4, j)
            if f % 4:
                halo = pltpu.roll(halo, LANES - spread * (f % 4), 1)
            whole.append(jnp.concatenate(parts + [halo], axis=1))
        for f in range(3):
            ahead[f, j] = whole[f]
            current[f, j] = whole[f]
            ends[f, j] = whole[f][:, :width]
            coefs[f, j] = whole[3 + f]
        one_re, one_im = whole[4], -whole[5]
        power_re, power_im = one_re, one_im
        for _ in range(FINE - 1):
            power_re, power_im = (
                power_re * one_re - power_im * one_im, power_re * one_im + power_im * one_re
            )
        coefs[3, j] = power_re
        coefs[4, j] = power_im

    def across_rows(a):
        first = pltpu.roll(a[0], SUBLANES - 1, 0)[None]
        last = pltpu.roll(a[-1], 1, 0)[None]
        return jnp.concatenate([a[1:], first], axis=0) - jnp.concatenate([last, a[:-1]], axis=0)

    def across_columns(a):
        return pltpu.roll(a, lanes - 1, 2) - pltpu.roll(a, 1, 2)

    def fine_step(state):
        height, along_x, along_y = state
        depth, cosine, sine = coefs[0], coefs[1], coefs[2]
        height = height - (across_rows(depth * along_x) + across_columns(depth * along_y))
        new_x = cosine * along_x + sine * along_y - across_rows(height)
        new_y = cosine * along_y - sine * along_x - across_columns(height)
        return height, new_x, new_y

    def coarse(state, part):
        height, along_x, along_y = state
        power_re, power_im = coefs[3, :, :, :part], coefs[4, :, :, :part]
        return (
            height,
            power_re * along_x - power_im * along_y,
            power_im * along_x + power_re * along_y,
        )

    def end_copy(local, target, source, t):
        offset = source * width + t * LANES
        return pltpu.make_async_remote_copy(
            src_ref=outgoing.at[local, :, t, pl.ds(pl.multiple_of(target * strip, strip), strip), :],
            dst_ref=out_ref.at[0, :, :, pl.ds(pl.multiple_of(offset, LANES), LANES)],
            send_sem=out_send.at[local, target, t],
            recv_sem=out_recv.at[source, t],
            device_id=(group * members + local, target),
            device_id_type=MESH,
        )

    def one_slice(n, carry):
        a = (ahead[0], ahead[1], ahead[2])
        b = (current[0], current[1], current[2])
        fine_a, fine_b = a, b
        for _ in range(FINE):
            fine_a, fine_b = fine_step(fine_a), fine_step(fine_b)
        coarse_a, coarse_b = coarse(a, lanes), coarse(b, lanes)
        ended = coarse((ends[0], ends[1], ends[2]), width)
        ended = [
            e + (f[:, :, :width] - g[:, :, :width]) for e, f, g in zip(ended, fine_b, coarse_b)
        ]
        for f in range(3):
            current[f] = coarse_b[f] + (fine_a[f] - coarse_a[f])
            ends[f] = ended[f]
        ahead[1] = coarse_a[1]
        ahead[2] = coarse_a[2]

        @pl.when(n >= group * members)
        def _():
            local = n - group * members
            for f in range(3):
                value = ended[f] * (1.0 / half_step) if f == 0 else ended[f]
                for j in range(groups_of_rows):
                    for t in range(tiles):
                        outgoing[local, f, t, pl.ds(j, SUBLANES, stride=groups_of_rows), :] = (
                            value[j, :, t * LANES:(t + 1) * LANES]
                        )
            for away in range(space):
                target = lax.rem(place + away, space)
                if away == 0:
                    @pl.when(local == member)
                    def _():
                        for t in range(tiles):
                            offset = block * width + t * LANES
                            for f in range(3):
                                out_ref[0, f, :, pl.ds(pl.multiple_of(offset, LANES), LANES)] = outgoing[
                                    local, f, t, pl.ds(pl.multiple_of(place * strip, strip), strip), :
                                ]

                    @pl.when(local != member)
                    def _():
                        for t in range(tiles):
                            end_copy(local, target, block, t).start()
                else:
                    for t in range(tiles):
                        end_copy(local, target, block, t).start()

        return carry

    lax.fori_loop(0, (group + 1) * members, one_slice, 0)

    for away in range(1, peers):
        peer = lax.rem(block + away, peers)
        for t in range(tiles):
            end_copy(lax.div(peer, space), lax.rem(peer, space), peer, t).wait_recv()
    for away in range(1, peers):
        peer = lax.rem(block + away, peers)
        for t in range(tiles):
            end_copy(lax.div(peer, space), lax.rem(peer, space), block, t).wait_send()
    for k in others:
        strip_copy(k, place).wait_send()


def on_device(sizes, start_state, still_depth, coriolis, drag_rate):
    tm_size, space, members, strip, columns = sizes
    width = columns // (space * members)
    tiles = width // LANES
    lanes = width + LANES
    rows = space * strip
    slabs = rows // SUBLANES
    peers = space * members
    staged = 6 * tiles + 2
    f32 = jnp.float32
    return pl.pallas_call(
        functools.partial(kernel, sizes),
        out_shape=jax.ShapeDtypeStruct((1, 3, strip, columns), f32),
        in_specs=[pl.BlockSpec(memory_space=pl.ANY)] * 4,
        out_specs=pl.BlockSpec(memory_space=pltpu.VMEM),
        scratch_shapes=[
            pltpu.VMEM((3, strip, columns), f32),
            pltpu.VMEM((strip, columns), f32),
            pltpu.VMEM((strip, columns), f32),
            pltpu.VMEM((strip, columns), f32),
            pltpu.VMEM((space, staged, strip, LANES), f32),
            pltpu.VMEM((staged, rows, LANES), f32),
            pltpu.VMEM((5, slabs, SUBLANES, lanes), f32),
            pltpu.VMEM((3, slabs, SUBLANES, lanes), f32),
            pltpu.VMEM((3, slabs, SUBLANES, lanes), f32),
            pltpu.VMEM((3, slabs, SUBLANES, width), f32),
            pltpu.VMEM((members, 3, tiles, rows, LANES), f32),
            pltpu.SemaphoreType.DMA((4,)),
            pltpu.SemaphoreType.DMA((space,)),
            pltpu.SemaphoreType.DMA((space,)),
            pltpu.SemaphoreType.DMA((members, space, tiles)),
            pltpu.SemaphoreType.DMA((peers, tiles)),
        ],
        compiler_params=pltpu.CompilerParams(collective_id=0, has_side_effects=True),
    )(start_state, still_depth, coriolis, drag_rate)


def solution(mesh):
    tm_size, space = mesh.shape["tm"], mesh.shape["space"]

    def body(start_state, still_depth, coriolis, drag_rate):
        strip, columns = still_depth.shape
        assert 2 * FINE * ITERS <= LANES // 8 and strip % SUBLANES == 0
        members = members_of(tm_size, space, columns)
        sizes = (tm_size, space, members, strip, columns)
        return on_device(sizes, start_state, still_depth, coriolis, drag_rate)

    placed = (P(None, "space", None), P("space", None), P("space", None), P("space", None))
    return jax.shard_map(
        body,
        mesh=mesh,
        in_specs=placed,
        out_specs=P("tm", None, "space", None),
        check_vma=False,
    )
```

time: 217 us -> 19.2 us (0.09)
  blocking collectives: 142 us -> 0 us
  waiting for transfers between devices: 35.4 us -> 0 us
  starting transfers between devices: 25.9 us -> 0 us
  Pallas kernels: 0 us -> 17.4 us
  other arithmetic: 7.95 us -> 0 us
  local copies, waits for them, and re-layouts: 4.33 us -> 1.62 us
    all_gather x8 -> x0, blocking collectives: 142 us -> none  [carried_in(): gathered = jax.tree.map(lambda a: lax.all_gather(a, axis), part)]
    ppermute x32 -> x0, waiting for transfers between devices: 35.4 us -> none  [the longest x16 22.2 us: with_halo(): before = lax.ppermute(last, axis, up)]
    ppermute x32 -> x0, starting transfers between devices: 25.9 us -> none  [the longest x16 13.6 us: with_halo(): before = lax.ppermute(last, axis, up)]
    pallas_call x0 -> x1, Pallas kernels: none -> 17.4 us  [on_device(): pl.pallas_call(functools.partial(kernel, sizes), out_shape=jax.ShapeDtype...]
    slice x52 -> x0, local copies, waits for them, and re-layouts: 3.17 us -> none  [the longest x16 1.21 us: step_margins(): slope_y = (jnp.roll(height_new, -1, 1) - jnp.roll(height_new, 1, 1)) * 0.5]
    mul x10 -> x0, other arithmetic: 2.66 us -> none  [the longest x8 1.96 us: step_margins(): flux_y = still_depth * along_y]
    another operation x5 -> x0, other arithmetic: 2.5 us -> none  [the longest x4 2.19 us: rotate(): return jnp.stack([height, turned_x, turned_y], axis=-3)]
  transfers between devices with their start and end apart: 32 -> 0, of which waited for: 30 -> 0; matrix products, arithmetic and copies ran while one was open for 1% -> 0% of each run, Pallas kernels for 0% -> 0%
where the time goes in v1:
time: 19.2 us; the launch traced here: 19.1 us
  Pallas kernels  17.4 us (91%)
  local copies, waits for them, and re-layouts  1.62 us (8%)
    pallas_call x1, Pallas kernels, on_device(): pl.pallas_call(functools.partial(kernel, sizes), out_shape=jax.ShapeDtype...  17.4 us
    unnamed x1, local copies, waits for them, and re-layouts  1.62 us

profile of v1, /device:TPU:25, one launch (start us, length us, event | category | flops | bytes accessed | tf_op | source)
XLA Modules:
  0.0 19.1 jit_solution(5365038711015078126)
XLA Ops:
  0.0 17.4 %shard_map.46 = f32[1,3,8,2048]{3,2,1,0:T(8,128)} custom-call(f32[3,8,2048]{2,1,0:T(8,128)} %start_ref.1, f32[8,2048]{1,0:T(8,128)} %depth_ref.1, f32[8,2048]{1,0:T(8,128)} %coriolis_ref.1, f32[8,2048]{1,0:T(8,128)} %drag_ref.1), custom_call_target="tpu_custom_call" | custom-call | tf_op jit(solution)/shard_map/pallas_call | solution.py:258
  17.4 1.6 %copy.6 = f32[1,3,8,2048]{3,2,1,0:T(8,128)} copy(f32[1,3,8,2048]{3,2,1,0:T(8,128)} %shard_map.46) | data formatting | bytes 393216

commit v2 on v1

--- a/solution.py
+++ b/solution.py
@@ -257,7 +257,7 @@
     f32 = jnp.float32
     return pl.pallas_call(
         functools.partial(kernel, sizes),
-        out_shape=jax.ShapeDtypeStruct((1, 3, strip, columns), f32),
+        out_shape=pltpu.VMEM((1, 3, strip, columns), f32),
         in_specs=[pl.BlockSpec(memory_space=pl.ANY)] * 4,
         out_specs=pl.BlockSpec(memory_space=pltpu.VMEM),
         scratch_shapes=[

time: 19.2 us -> 17.6 us (0.917)
  local copies, waits for them, and re-layouts: 1.62 us -> 0.68 us
  Pallas kernels: 17.4 us -> 16.8 us
    unnamed x1, local copies, waits for them, and re-layouts: 1.62 us -> 0.68 us
    pallas_call x1, Pallas kernels: 17.4 us -> 16.8 us  [on_device(): pl.pallas_call(functools.partial(kernel, sizes), out_shape=pltpu.VMEM((1,...]
where the time goes in v2:
time: 17.6 us; the launch traced here: 17.4 us
  Pallas kernels  16.8 us (95%)
  local copies, waits for them, and re-layouts  0.68 us (4%)
    pallas_call x1, Pallas kernels, on_device(): pl.pallas_call(functools.partial(kernel, sizes), out_shape=pltpu.VMEM((1,...  16.8 us
    unnamed x1, local copies, waits for them, and re-layouts  0.68 us

profile of v2, /device:TPU:25, one launch (start us, length us, event | category | flops | bytes accessed | tf_op | source)
XLA Modules:
  0.0 17.4 jit_solution(15169918585162295383)
XLA Ops:
  0.0 16.8 %shard_map.46 = f32[1,3,8,2048]{3,2,1,0:T(8,128)S(1)} custom-call(f32[3,8,2048]{2,1,0:T(8,128)} %start_ref.1, f32[8,2048]{1,0:T(8,128)} %depth_ref.1, f32[8,2048]{1,0:T(8,128)} %coriolis_ref.1, f32[8,2048]{1,0:T(8,128)} %drag_ref.1), custom_call_target="tpu_custom_call" | custom-call | tf_op jit(solution)/shard_map/pallas_call | solution.py:258
  16.8 0.7 %copy.6 = f32[1,3,8,2048]{3,2,1,0:T(8,128)} copy(f32[1,3,8,2048]{3,2,1,0:T(8,128)S(1)} %shard_map.46) | data formatting | bytes 393216

commit v3 on v2

--- a/solution.py
+++ b/solution.py
@@ -26,9 +26,15 @@
     return best
 
 
+def far_first(index, count):
+    if count & (count - 1):
+        return [lax.rem(index + away, count) for away in range(1, count + 1)]
+    return [jnp.bitwise_xor(index, away) for away in range(count - 1, -1, -1)]
+
+
 def kernel(
     sizes, start_ref, depth_ref, coriolis_ref, drag_ref, out_ref,
-    state_in, depth_in, coriolis_in, drag_in, stage, recv, coefs, ahead, current, ends, outgoing,
+    state_in, depth_in, coriolis_in, drag_in, stage, recv, coefs, ahead, current, ends, jumps, outgoing,
     load_sem, in_send, in_recv, out_send, out_recv,
 ):
     tm_size, space, members, strip, columns = sizes
@@ -115,7 +121,7 @@
             device_id_type=MESH,
         )
 
-    others = [lax.rem(place + away, space) for away in range(1, space)]
+    others = far_first(place, space)[:-1]
     for k in others:
         strip_copy(k, place).start()
     for k in others:
@@ -182,56 +188,83 @@
             device_id_type=MESH,
         )
 
-    def one_slice(n, carry):
-        a = (ahead[0], ahead[1], ahead[2])
-        b = (current[0], current[1], current[2])
-        fine_a, fine_b = a, b
+    def fine(states):
         for _ in range(FINE):
-            fine_a, fine_b = fine_step(fine_a), fine_step(fine_b)
-        coarse_a, coarse_b = coarse(a, lanes), coarse(b, lanes)
-        ended = coarse((ends[0], ends[1], ends[2]), width)
-        ended = [
-            e + (f[:, :, :width] - g[:, :, :width]) for e, f, g in zip(ended, fine_b, coarse_b)
-        ]
+            states = [fine_step(state) for state in states]
+        return states
+
+    def first_jumps(batch, carry, count=members):
+        state = (ahead[0], ahead[1], ahead[2])
+        starts = []
+        for _ in range(count):
+            starts.append(state)
+            state = coarse(state, lanes)
+        ahead[1], ahead[2] = state[1], state[2]
+        after = starts[1:] + [state]
+        for i, (ended, turned) in enumerate(zip(fine(starts), after)):
+            for f in range(3):
+                jumps[batch * members + i, f] = ended[f] - turned[f]
+        return carry
+
+    def last_ends(batch, carry, known=0):
+        state = (current[0], current[1], current[2])
+        starts, turned = [], []
+        for i in range(members):
+            starts.append(state)
+            turned.append(coarse(state, lanes))
+            state = [turned[i][f] + jumps[batch * members + i, f] for f in range(3)]
         for f in range(3):
-            current[f] = coarse_b[f] + (fine_a[f] - coarse_a[f])
+            current[f] = state[f]
+        ended = (ends[0], ends[1], ends[2])
+        fine_ends = [None] * known + fine(starts[known:])
+        for i, fine_end in enumerate(fine_ends):
+            ended = coarse(ended, width)
+            if fine_end is None:
+                jump = [jumps[i, f, :, :, :width] for f in range(3)]
+            else:
+                jump = [f[:, :, :width] - g[:, :, :width] for f, g in zip(fine_end, turned[i])]
+            ended = [e + a for e, a in zip(ended, jump)]
+
+            @pl.when(batch == group)
+            def _():
+                put(i, ended)
+
+        for f in range(3):
             ends[f] = ended[f]
-        ahead[1] = coarse_a[1]
-        ahead[2] = coarse_a[2]
-
-        @pl.when(n >= group * members)
+
+        @pl.when(batch == group)
         def _():
-            local = n - group * members
-            for f in range(3):
-                value = ended[f] * (1.0 / half_step) if f == 0 else ended[f]
-                for j in range(groups_of_rows):
-                    for t in range(tiles):
-                        outgoing[local, f, t, pl.ds(j, SUBLANES, stride=groups_of_rows), :] = (
-                            value[j, :, t * LANES:(t + 1) * LANES]
-                        )
-            for away in range(space):
-                target = lax.rem(place + away, space)
-                if away == 0:
-                    @pl.when(local == member)
-                    def _():
-                        for t in range(tiles):
-                            offset = block * width + t * LANES
-                            for f in range(3):
-                                out_ref[0, f, :, pl.ds(pl.multiple_of(offset, LANES), LANES)] = outgoing[
-                                    local, f, t, pl.ds(pl.multiple_of(place * strip, strip), strip), :
-                                ]
-
-                    @pl.when(local != member)
-                    def _():
-                        for t in range(tiles):
-                            end_copy(local, target, block, t).start()
-                else:
+            send()
+
+        return carry
+
+    def put(local, ended):
+        for f in range(3):
+            value = ended[f] * (1.0 / half_step) if f == 0 else ended[f]
+            for j in range(groups_of_rows):
+                for t in range(tiles):
+                    outgoing[local, f, t, pl.ds(j, SUBLANES, stride=groups_of_rows), :] = (
+                        value[j, :, t * LANES:(t + 1) * LANES]
+                    )
+
+    def send():
+        locals_, targets = far_first(member, members), far_first(place, space)
+        for a, local in enumerate(locals_):
+            for b, target in enumerate(targets):
+                if (a, b) != (members - 1, space - 1):
                     for t in range(tiles):
                         end_copy(local, target, block, t).start()
-
-        return carry
-
-    lax.fori_loop(0, (group + 1) * members, one_slice, 0)
+        for t in range(tiles):
+            offset = block * width + t * LANES
+            for f in range(3):
+                out_ref[0, f, :, pl.ds(pl.multiple_of(offset, LANES), LANES)] = outgoing[
+                    member, f, t, pl.ds(pl.multiple_of(place * strip, strip), strip), :
+                ]
+
+    lax.fori_loop(0, group, first_jumps, 0)
+    first_jumps(group, 0, max(members - 1, 1))
+    last_ends(0, 0, 1)
+    lax.fori_loop(1, group + 1, last_ends, 0)
 
     for away in range(1, peers):
         peer = lax.rem(block + away, peers)
@@ -271,6 +304,7 @@
             pltpu.VMEM((3, slabs, SUBLANES, lanes), f32),
             pltpu.VMEM((3, slabs, SUBLANES, lanes), f32),
             pltpu.VMEM((3, slabs, SUBLANES, width), f32),
+            pltpu.VMEM((tm_size, 3, slabs, SUBLANES, lanes), f32),
             pltpu.VMEM((members, 3, tiles, rows, LANES), f32),
             pltpu.SemaphoreType.DMA((4,)),
             pltpu.SemaphoreType.DMA((space,)),

time: 17.6 us -> 15.7 us (0.89)
  the two profiles are of different devices: /device:TPU:25 before, /device:TPU:16 now
where the time goes in v3:
time: 15.7 us; the launch traced here: 15.6 us
  Pallas kernels  14.9 us (95%)
  local copies, waits for them, and re-layouts  0.68 us (4%)
    pallas_call x1, Pallas kernels, on_device(): pl.pallas_call(functools.partial(kernel, sizes), out_shape=pltpu.VMEM((1,...  14.9 us
    unnamed x1, local copies, waits for them, and re-layouts  0.68 us

profile of v3, /device:TPU:16, one launch (start us, length us, event | category | flops | bytes accessed | tf_op | source)
XLA Modules:
  0.0 15.6 jit_solution(12468636451052863323)
XLA Ops:
  0.0 14.9 %shard_map.46 = f32[1,3,8,2048]{3,2,1,0:T(8,128)S(1)} custom-call(f32[3,8,2048]{2,1,0:T(8,128)} %start_ref.1, f32[8,2048]{1,0:T(8,128)} %depth_ref.1, f32[8,2048]{1,0:T(8,128)} %coriolis_ref.1, f32[8,2048]{1,0:T(8,128)} %drag_ref.1), custom_call_target="tpu_custom_call" | custom-call | tf_op jit(solution)/shard_map/pallas_call | solution.py:291
  14.9 0.7 %copy.6 = f32[1,3,8,2048]{3,2,1,0:T(8,128)} copy(f32[1,3,8,2048]{3,2,1,0:T(8,128)S(1)} %shard_map.46) | data formatting | bytes 393216
